TPU v7x, 32 devices: a whole 2x2x4 slice. The times are simulated.
32 devices in a mesh: mem: 4 (over y, x), tile: 8 (over z, core).
Axes of the slice: x: 2, y: 2, z: 4, core: 2. Of those that a mesh axis runs over, the one named last changes fastest.
Arguments:
- members: float32 [40, 2, 65536], P('mem', None, 'tile'), may hold values from -6 to 6
- increment: float32 [2, 262144], P(None, 'tile'), may hold values from -6 to 6
- fine_angles: float32 [2, 262144], P(None, 'tile'), may hold values from -1.5 to 1.5
- coarse_angles: float32 [2, 65536], P(None, 'tile'), may hold values from -1.5 to 1.5
- remap_weights: bfloat16 [8, 64, 4, 256, 128], P('tile', 'mem'), may hold values from -0.1875 to 0.1875
- sources: int32 [8, 64, 4], P('tile', 'mem'), may hold values from 0 to 1023, as said below
- counts: int32 [8, 64], P('tile', 'mem'), may hold values from 2 to 4, as said below
Outputs:
- recentered: float32 [40, 2, 65536], P('mem', None, 'tile')
Inputs may be any that keep to these rules, and one draw needn't show every extreme that they name: `sources`: for entry [s, l], with g = 64 s + l, slots 0 and 1 name fine blocks 2 g and 2 g + 1; each further even slot names block (2 g - r) mod 1024 and each further odd slot block (2 g + 1 + r + 512) mod 1024, each with its own r from 1 to 128. `counts`: every column shard holds a coarse block that uses all 4 slots.
All inputs are finite; a program needn't handle non-finite values.
Results may differ from a plain program's by a relative error of at most 0.0017.
Values may be sent and summed in bfloat16 or wider, within the bound.
A program may use at most 64 MiB of HBM per device.

v0:
```python
import jax
import jax.numpy as jnp
from jax import lax
from jax.sharding import PartitionSpec as P


def shifted(value, axis, by):
    length = lax.axis_size(axis)
    return lax.ppermute(value, axis, [(i, (i + by) % length) for i in range(length)])


def to_vector(east_part, north_part, longitude, latitude):
    sin_lon, cos_lon = (jnp.sin(longitude), jnp.cos(longitude))
    sin_lat, cos_lat = (jnp.sin(latitude), jnp.cos(latitude))
    first = -sin_lon * east_part - sin_lat * cos_lon * north_part
    second = cos_lon * east_part - sin_lat * sin_lon * north_part
    third = cos_lat * north_part
    return (first, second, third)


def to_wind(first, second, third, longitude, latitude):
    sin_lon, cos_lon = (jnp.sin(longitude), jnp.cos(longitude))
    sin_lat, cos_lat = (jnp.sin(latitude), jnp.cos(latitude))
    east_part = -sin_lon * first + cos_lon * second
    north_part = -sin_lat * cos_lon * first - sin_lat * sin_lon * second + cos_lat * third
    return jnp.stack([east_part, north_part])


def shards(members, increment, fine_angles, coarse_angles, remap_weights, sources, counts):
    weights = remap_weights[0]
    source_ids = sources[0]
    slot_counts = counts[0]
    block_count = source_ids.shape[0]
    slot_total = source_ids.shape[1]
    fine_width = weights.shape[2]
    coarse_width = weights.shape[3]
    fine_blocks = increment.shape[1] // fine_width
    tile_index = lax.axis_index("tile")
    mem_index = lax.axis_index("mem")
    first, second, third = to_vector(
        increment[0].reshape(fine_blocks, fine_width),
        increment[1].reshape(fine_blocks, fine_width),
        fine_angles[0].reshape(fine_blocks, fine_width),
        fine_angles[1].reshape(fine_blocks, fine_width),
    )
    flat_blocks = (
        jnp.stack([first, second, third], axis=1)
        .astype(jnp.bfloat16)
        .reshape(fine_blocks, 3 * fine_width)
    )
    row_width = flat_blocks.shape[1]
    far_ids = source_ids[:, 2:].reshape(-1)
    far_count = far_ids.shape[0]
    peer_count = lax.axis_size("tile")
    half = peer_count // 2

    def serve(asked_ids):
        taken = jnp.take(flat_blocks, jnp.clip(asked_ids, 0, fine_blocks - 1), axis=0)
        return jnp.where((asked_ids >= 0)[:, None], taken, jnp.zeros_like(taken))

    below_ids = source_ids[:, 2::2].reshape(-1)
    below_owner = below_ids // fine_blocks
    below_local = below_ids - below_owner * fine_blocks
    lower_shard = (tile_index + peer_count - 1) % peer_count
    ask_low = jnp.where(below_owner == lower_shard, below_local, -1)
    asked_low = shifted(ask_low, "tile", -1)
    lower_rows = shifted(serve(asked_low), "tile", 1)
    is_own = below_owner == tile_index
    own_rows = serve(jnp.where(is_own, below_local, -1))
    below_rows = jnp.where(is_own[:, None], own_rows, lower_rows)
    across_ids = source_ids[:, 3::2].reshape(-1)
    across_owner = across_ids // fine_blocks
    across_local = across_ids - across_owner * fine_blocks
    half_shard = (tile_index + half) % peer_count
    beyond_shard = (tile_index + half + 1) % peer_count
    ask_half = jnp.where(across_owner == half_shard, across_local, -1)
    asked_half = shifted(ask_half, "tile", half)
    half_rows = shifted(serve(asked_half), "tile", -half)
    ask_next = jnp.where(across_owner == beyond_shard, across_local, -1)
    asked_next = shifted(ask_next, "tile", half + 1)
    next_rows = shifted(serve(asked_next), "tile", -(half + 1))
    across_rows = jnp.where((across_owner == half_shard)[:, None], half_rows, next_rows)
    pairs = (slot_total - 2) // 2
    fetched = jnp.stack(
        [
            below_rows.reshape(block_count, pairs, row_width),
            across_rows.reshape(block_count, pairs, row_width),
        ],
        axis=2,
    )
    fetched = fetched.reshape(far_count, row_width)
    near_ids = source_ids[:, :2].reshape(-1) - tile_index * fine_blocks
    near_rows = jnp.take(flat_blocks, near_ids, axis=0)
    picked = jnp.concatenate(
        [near_rows.reshape(block_count, 2, -1), fetched.reshape(block_count, slot_total - 2, -1)],
        axis=1,
    )
    picked = picked.reshape(block_count, slot_total, 3, fine_width)
    live_slots = jnp.arange(slot_total, dtype=jnp.int32)[None, :] < slot_counts[:, None]
    picked = jnp.where(live_slots[:, :, None, None], picked, 0)
    coarse_cart = jnp.einsum("ikcf,ikfb->cib", picked, weights, preferred_element_type=jnp.float32)
    coarse_cart = coarse_cart.reshape(3, block_count * coarse_width)
    own_columns = block_count * coarse_width
    own_angles = lax.dynamic_slice_in_dim(coarse_angles, mem_index * own_columns, own_columns, 1)
    own_wind = to_wind(coarse_cart[0], coarse_cart[1], coarse_cart[2], own_angles[0], own_angles[1])
    member_count = members.shape[0] * lax.axis_size("mem")
    coarse_wind = lax.all_gather(own_wind, "mem", axis=1, tiled=True)
    member_total = lax.psum(jnp.sum(members, axis=0), "mem")
    member_mean = member_total / member_count
    return members - member_mean[None] + coarse_wind[None]


def solution(mesh):
    in_specs = (
        P("mem", None, "tile"),
        P(None, "tile"),
        P(None, "tile"),
        P(None, "tile"),
        P("tile", "mem", None, None, None),
        P("tile", "mem", None),
        P("tile", "mem"),
    )
    out_specs = P("mem", None, "tile")
    return jax.shard_map(shards, mesh=mesh, in_specs=in_specs, out_specs=out_specs, check_vma=False)
```

profile of v0, /device:TPU:0, one launch (start us, length us, event | category | flops | bytes accessed | tf_op | source)
XLA Modules:
  0.0 67.5 jit_solution(10201387090370260381)
XLA Ops:
  6.5 0.0 copy-start.1
  6.5 0.0 copy-start.2
  6.5 0.0 all-reduce.2.cloned.1.call-start
  6.5 0.8 %compare_and_fusion.3 = (pred[16]{0:T(512)(128)(4,1)S(1)}, s32[16]{0:T(128)S(1)}, s32[16]{0:T(128)S(1)}) fusion(s32[16,4]{0,1:T(4,128)} %bitcast.73, s32[]{:T(128)S(6)} %axis_index.25), kind=kLoop, calls=%fused_computation.58 | loop fusion | flops 416 | bytes 212 | tf_op jit(solution)/shard_map/jit(_take)/and | solution.py:58
  7.3 0.8 %compare_select_fusion.6 = (s32[16]{0:T(128)S(1)}, s32[16]{0:T(128)S(1)}, s32[16]{0:T(128)S(1)}) fusion(s32[]{:T(128)S(6)} %select_n.119, s32[16,4]{0,1:T(4,128)} %bitcast.74, s32[16]{0:T(128)S(1)} %get-tuple-element.18, s32[]{:T(128)S(6)} %select_n.110), kind=kLoop, calls=%fused_computation.59 | loop fusion | flops 368 | bytes 392 | tf_op jit(solution)/shard_map/jit(_where)/select_n | solution.py:79
  8.1 0.7 %compare_select_fusion.7 = s32[16]{0:T(128)S(1)} fusion(s32[16]{0:T(128)S(1)} %get-tuple-element.24, s32[]{:T(128)S(6)} %select_n.115, s32[16,4]{0,1:T(4,128)} %bitcast.75), kind=kLoop, calls=%fused_computation.60 | loop fusion | flops 64 | bytes 196 | tf_op jit(solution)/shard_map/jit(_where)/select_n | solution.py:76
  8.8 4.1 %collective-permute-start.2 = (s32[16]{0:T(128)S(1)}, s32[16]{0:T(128)S(1)}, u32[]{:S(2)}, u32[]{:S(2)}) collective-permute-start(s32[16]{0:T(128)S(1)} %compare_select_fusion.7), channel_id=1, source_target_pairs={{0,4},{1,5},{2,6},{3,7},{4,0},{5,1},{6,2},{7,3},{8,12},{9,13},{10,... | collective-permute-start | bytes 200 | tf_op jit(solution)/shard_map/ppermute | solution.py:9
  12.9 0.0 collective-permute-start.4
  12.9 1.2 %collective-permute-start = (s32[16]{0:T(128)S(1)}, s32[16]{0:T(128)S(1)}, u32[]{:S(2)}, u32[]{:S(2)}) collective-permute-start(s32[16]{0:T(128)S(1)} %get-tuple-element.34), channel_id=1, source_target_pairs={{0,7},{1,0},{2,1},{3,2},{4,3},{5,4},{6,5},{7,6},{8,15},{9,8},{10,9... | collective-permute-start | bytes 200 | tf_op jit(solution)/shard_map/ppermute | solution.py:9
  14.1 1.9 %reduce_sum.9 = f32[2,8192]{1,0:T(2,128)} reduce(f32[10,2,8192]{2,1,0:T(2,128)} %param.9, f32[]{:T(128)} %constant.81.clone.1), dimensions={0}, to_apply=%region_0.1 | reduce | flops 147456 | bytes 720900 | tf_op jit(solution)/shard_map/reduce_sum | solution.py:108
  16.0 0.0 all-reduce.2.cloned.1.call-update
  16.0 0.7 %compare_bitcast_fusion.2 = (pred[16]{0:T(512)(128)(4,1)S(1)}, s32[16,1]{0,1:T(1,128)S(1)}) fusion(s32[]{:T(128)S(6)} %axis_index.25, s32[16,4]{0,1:T(4,128)} %bitcast.76), kind=kLoop, calls=%fused_computation.83 | loop fusion | flops 256 | bytes 148 | tf_op jit(solution)/shard_map/jit(_where)/broadcast_in_dim | solution.py:70
  16.7 1.7 %slice_reduce_fusion.1 = (f32[32768]{0:T(1024)S(1)}, f32[32768]{0:T(1024)S(1)}) fusion(f32[2,32768]{1,0:T(2,128)} %param.10), kind=kLoop, calls=%fused_computation.22 | loop fusion | bytes 524288 | tf_op jit(solution)/shard_map/slice | solution.py:41
  18.5 10.0 %cosine_reduce_fusion.1 = (f32[32768]{0:T(1024)S(1)}, f32[32768]{0:T(1024)S(1)}, f32[32768]{0:T(1024)S(1)}, f32[32768]{0:T(1024)S(1)}) fusion(f32[2,32768]{1,0:T(2,128)} %param.11), kind=kLoop, calls=%fused_computation.20 | loop fusion | bytes 786432 | tf_op jit(solution)/shard_map/cos | solution.py:13
  28.7 0.1 subtract_convert_fusion.1
  28.8 0.0 copy-start
  28.8 0.2 copy.34
  29.0 0.2 copy.36
  29.2 0.0 copy-done.1
  29.2 0.1 copy.35
  29.3 0.1 sub.80
  29.4 0.6 gather_fusion.1
  30.0 0.6 gather_fusion
  30.7 0.1 copy.33
  30.8 0.0 copy-done.2
  30.8 0.1 iota_compare_fusion
  30.9 0.1 broadcast_select_fusion
  31.0 0.0 collective-permute-done.2
  31.0 0.6 gather_fusion.3
  31.6 0.1 select_select_fusion.1
  31.7 2.0 %collective-permute-start.3 = (bf16[16,768]{1,0:T(8,128)(2,1)S(1)}, bf16[16,768]{1,0:T(8,128)(2,1)S(1)}, u32[]{:S(2)}, u32[]{:S(2)}) collective-permute-start(bf16[16,768]{1,0:T(8,128)(2,1)S(1)} %select_select_fusion.1), channel_id=1, source_target_pairs={{0,4},{1,5},{2,6},{3,7},{4,0},{5,1},{6,2},{7,3},{8,12},{9,13},{10,... | collective-permute-start | bytes 73736 | tf_op jit(solution)/shard_map/ppermute | solution.py:9
  33.7 0.0 collective-permute-done.4
  33.8 0.6 gather_fusion.4
  34.3 0.1 select_select_fusion
  34.4 0.3 collective-permute-start.5
  34.7 0.0 collective-permute-done
  34.7 0.6 gather_fusion.2
  35.3 0.1 select_select_fusion.2
  35.4 0.7 %collective-permute-start.1 = (bf16[16,768]{1,0:T(8,128)(2,1)S(1)}, bf16[16,768]{1,0:T(8,128)(2,1)S(1)}, u32[]{:S(2)}, u32[]{:S(2)}) collective-permute-start(bf16[16,768]{1,0:T(8,128)(2,1)S(1)} %select_select_fusion.2), channel_id=1, source_target_pairs={{0,1},{1,2},{2,3},{3,4},{4,5},{5,6},{6,7},{7,0},{8,9},{9,10},{10,1... | collective-permute-start | bytes 73736 | tf_op jit(solution)/shard_map/ppermute | solution.py:9
  36.2 0.3 collective-permute-done.3
  36.4 2.2 %collective-permute-done.5 = bf16[16,768]{1,0:T(8,128)(2,1)S(1)} collective-permute-done((bf16[16,768]{1,0:T(8,128)(2,1)S(1)}, bf16[16,768]{1,0:T(8,128)(2,1)S(1)}, u32[]{:S(2)}, u32[]{:S(2)}) %collective-permute-start.5) | collective-permute-done | bytes 24608 | tf_op jit(solution)/shard_map/ppermute | solution.py:9
  38.6 0.1 broadcast_select_fusion.1
  38.7 1.8 %collective-permute-done.1 = bf16[16,768]{1,0:T(8,128)(2,1)S(1)} collective-permute-done((bf16[16,768]{1,0:T(8,128)(2,1)S(1)}, bf16[16,768]{1,0:T(8,128)(2,1)S(1)}, u32[]{:S(2)}, u32[]{:S(2)}) %collective-permute-start.1) | collective-permute-done | bytes 24608 | tf_op jit(solution)/shard_map/ppermute | solution.py:9
  40.5 0.1 fusion.11
  40.6 2.9 %fusion.2 = f32[3,16,128]{2,0,1:T(4,128)S(1)} fusion(bf16[1,16,4,256,128]{4,3,2,1,0:T(8,128)(2,1)} %param.13, bf16[16,1,3,256]{3,2,1,0:T(4,128)(2,1)S(1)} %bitcast.71, bf16[16,1,3,256]{3,2,1,0:T(4,128)(2,1)S(1)} %bitcast.72, bf16[16,2,3,256]{3,2,1,0:T(4,128)(2,1)S(1)} %broadcast_select_fusion, pred[16,4]{1,0:T(8,128)(4,1)S(1)} %iota_compare_fusion), kind=kOutput, calls=%fused_computation.7 | convolution fusion | flops 12926976 | bytes 4317248 | tf_op jit(solution)/shard_map/ikcf,ikfb->cib/dot_general | solution.py:101
  43.5 1.3 %multiply_add_fusion = (f32[1,2048]{1,0:T(1,128)S(1)}, f32[1,2048]{1,0:T(1,128)S(1)}) fusion(f32[3,16,128]{2,0,1:T(4,128)S(1)} %fusion.2, f32[2,8192]{1,0:T(2,128)} %param.12, s32[]{:T(128)S(6)} %select_n.101, s32[]{:T(128)S(6)} %add.107), kind=kLoop, calls=%fused_computation.40 | loop fusion | flops 24576 | bytes 57352 | tf_op jit(solution)/shard_map/add | solution.py:24
  44.9 8.2 %all_gather.3 = f32[2,8192]{1,0:T(2,128)S(1)} all-gather(f32[2,2048]{1,0:T(2,128)S(1)} %pad_maximum_fusion.1), channel_id=1, replica_groups=mesh['mem'=4,'tile'=8] {'mem'}, dimensions={1}, use_global_device_ids=true | all-gather | bytes 81920 | tf_op jit(solution)/shard_map/all_gather | solution.py:107
  53.1 5.6 %all-reduce.2.cloned.1.call-done = f32[2,8192]{1,0:T(2,128)} async-done(((f32[2,8192]{1,0:T(2,128)}), f32[2,8192]{1,0:T(2,128)}) %all-reduce.2.cloned.1.call-update) | async-done | bytes 65552 | tf_op jit(solution)/shard_map/psum | solution.py:108
  58.7 0.9 %broadcast_multiply_fusion = f32[2,8192]{1,0:T(2,128)S(1)} fusion(f32[2,8192]{1,0:T(2,128)} %all-reduce.2.cloned.1.call-done), kind=kLoop, calls=%fused_computation.27 | loop fusion | flops 16384 | bytes 131072 | tf_op jit(solution)/shard_map/div | solution.py:109
  59.6 0.0 copy-done
  59.6 1.1 %subtract_add_fusion = f32[10,2,8192]{2,1,0:T(2,128)} fusion(f32[10,2,8192]{2,1,0:T(2,128)S(1)} %copy-done, f32[2,8192]{1,0:T(2,128)S(1)} %all_gather.3, f32[2,8192]{1,0:T(2,128)S(1)} %broadcast_multiply_fusion), kind=kLoop, calls=%fused_computation.8 | loop fusion | flops 327680 | bytes 1441792 | tf_op jit(solution)/shard_map/add | solution.py:110
  (22 shorter events, 0.4 us)
Async XLA Ops:
  6.5 22.6 %copy-start.1 = (s32[1,16,4]{1,2,0:T(4,128)S(1)}, s32[1,16,4]{1,2,0:T(4,128)}, u32[]{:S(2)}) copy-start(s32[1,16,4]{1,2,0:T(4,128)} %param.14) | copy-start | bytes 772
  6.5 24.2 %copy-start.2 = (s32[1,16]{1,0:T(1,128)S(1)}, s32[1,16]{1,0:T(1,128)}, u32[]{:S(2)}) copy-start(s32[1,16]{1,0:T(1,128)} %param.15) | copy-start | bytes 196
  6.5 52.1 %all-reduce.2.cloned.1.call-start = ((), (), s32[]{:S(2)}) async-start(), calls=%async_computation | async-start | bytes 131072 | tf_op jit(solution)/shard_map/psum | solution.py:108
  8.8 22.2 %collective-permute-start.2 = (s32[16]{0:T(128)S(1)}, s32[16]{0:T(128)S(1)}, u32[]{:S(2)}, u32[]{:S(2)}) collective-permute-start(s32[16]{0:T(128)S(1)} %compare_select_fusion.7), channel_id=1, source_target_pairs={{0,4},{1,5},{2,6},{3,7},{4,0},{5,1},{6,2},{7,3},{8,12},{9,13},{10,... | collective-permute-start | bytes 200 | tf_op jit(solution)/shard_map/ppermute | solution.py:9
  12.9 20.9 %collective-permute-start.4 = (s32[16]{0:T(128)S(1)}, s32[16]{0:T(128)S(1)}, u32[]{:S(2)}, u32[]{:S(2)}) collective-permute-start(s32[16]{0:T(128)S(1)} %get-tuple-element.23), channel_id=1, source_target_pairs={{0,5},{1,6},{2,7},{3,0},{4,1},{5,2},{6,3},{7,4},{8,13},{9,14},{10,... | collective-permute-start | bytes 200 | tf_op jit(solution)/shard_map/ppermute | solution.py:9
  12.9 21.9 %collective-permute-start = (s32[16]{0:T(128)S(1)}, s32[16]{0:T(128)S(1)}, u32[]{:S(2)}, u32[]{:S(2)}) collective-permute-start(s32[16]{0:T(128)S(1)} %get-tuple-element.34), channel_id=1, source_target_pairs={{0,7},{1,0},{2,1},{3,2},{4,3},{5,4},{6,5},{7,6},{8,15},{9,8},{10,9... | collective-permute-start | bytes 200 | tf_op jit(solution)/shard_map/ppermute | solution.py:9
  28.8 30.8 %copy-start = (f32[10,2,8192]{2,1,0:T(2,128)S(1)}, f32[10,2,8192]{2,1,0:T(2,128)}, u32[]{:S(2)}) copy-start(f32[10,2,8192]{2,1,0:T(2,128)} %param.9) | copy-start | bytes 1966084
  31.7 4.7 %collective-permute-start.3 = (bf16[16,768]{1,0:T(8,128)(2,1)S(1)}, bf16[16,768]{1,0:T(8,128)(2,1)S(1)}, u32[]{:S(2)}, u32[]{:S(2)}) collective-permute-start(bf16[16,768]{1,0:T(8,128)(2,1)S(1)} %select_select_fusion.1), channel_id=1, source_target_pairs={{0,4},{1,5},{2,6},{3,7},{4,0},{5,1},{6,2},{7,3},{8,12},{9,13},{10,... | collective-permute-start | bytes 73736 | tf_op jit(solution)/shard_map/ppermute | solution.py:9
  34.4 4.2 %collective-permute-start.5 = (bf16[16,768]{1,0:T(8,128)(2,1)S(1)}, bf16[16,768]{1,0:T(8,128)(2,1)S(1)}, u32[]{:S(2)}, u32[]{:S(2)}) collective-permute-start(bf16[16,768]{1,0:T(8,128)(2,1)S(1)} %select_select_fusion), channel_id=1, source_target_pairs={{0,3},{1,4},{2,5},{3,6},{4,7},{5,0},{6,1},{7,2},{8,11},{9,12},{10,... | collective-permute-start | bytes 73736 | tf_op jit(solution)/shard_map/ppermute | solution.py:9
  35.4 5.1 %collective-permute-start.1 = (bf16[16,768]{1,0:T(8,128)(2,1)S(1)}, bf16[16,768]{1,0:T(8,128)(2,1)S(1)}, u32[]{:S(2)}, u32[]{:S(2)}) collective-permute-start(bf16[16,768]{1,0:T(8,128)(2,1)S(1)} %select_select_fusion.2), channel_id=1, source_target_pairs={{0,1},{1,2},{2,3},{3,4},{4,5},{5,6},{6,7},{7,0},{8,9},{9,10},{10,1... | collective-permute-start | bytes 73736 | tf_op jit(solution)/shard_map/ppermute | solution.py:9
Sparse Core Ops, SparseCore 0:
  16.1 42.4 all-reduce.1
where the time goes:
time: 68 us; the launch traced here: 67.5 us
  local copies, waits for them, and re-layouts  15.6 us (23%)
  between operations  13.7 us (20%)
  waiting for transfers between devices  9.8 us (14%)
  other arithmetic  8.94 us (13%)
  starting transfers between devices  8.33 us (12%)
  blocking collectives  8.25 us (12%)
  matrix products  2.94 us (4%)
    cos x2, local copies, waits for them, and re-layouts, to_vector(): sin_lon, cos_lon = (jnp.sin(longitude), jnp.cos(longitude))  10 us
    ppermute x6, starting transfers between devices, shifted(): lax.ppermute(value, axis, [(i, (i + by) % length) for i in range(length)])  8.33 us
    all_gather x1, blocking collectives, shards(): coarse_wind = lax.all_gather(own_wind, 'mem', axis=1, tiled=True)  8.25 us
    psum x1, waiting for transfers between devices, shards(): member_total = lax.psum(jnp.sum(members, axis=0), 'mem')  5.56 us
    ppermute x6, waiting for transfers between devices, shifted(): lax.ppermute(value, axis, [(i, (i + by) % length) for i in range(length)])  4.23 us
    dot_general x1, matrix products, shards(): jnp.einsum('ikcf,ikfb->cib', picked, weights, preferred_element_type=jnp....  2.94 us
    gather x4, local copies, waits for them, and re-layouts, serve(): jnp.take(flat_blocks, jnp.clip(asked_ids, 0, fine_blocks - 1), axis=0)  2.36 us
    reduce_sum x1, other arithmetic, shards(): member_total = lax.psum(jnp.sum(members, axis=0), 'mem')  1.94 us
  transfers between devices with their start and end apart: 7, of which 4 were waited for; matrix products, arithmetic and copies ran while one was open for 34% of the time, Pallas kernels for 0%

commit v1 on v0

v1 whole, which is shorter than its diff:
```python
import functools

import jax
import jax.numpy as jnp
from jax import lax
from jax.experimental import pallas as pl
from jax.experimental.pallas import tpu as pltpu
from jax.sharding import PartitionSpec as P

LANES = 128
MESH = pl.DeviceIdType.MESH


def to_vector(east_part, north_part, longitude, latitude):
    sin_lon, cos_lon = (jnp.sin(longitude), jnp.cos(longitude))
    sin_lat, cos_lat = (jnp.sin(latitude), jnp.cos(latitude))
    first = -sin_lon * east_part - sin_lat * cos_lon * north_part
    second = cos_lon * east_part - sin_lat * sin_lon * north_part
    third = cos_lat * north_part
    return (first, second, third)


def to_wind(first, second, third, longitude, latitude):
    sin_lon, cos_lon = (jnp.sin(longitude), jnp.cos(longitude))
    sin_lat, cos_lat = (jnp.sin(latitude), jnp.cos(latitude))
    east_part = -sin_lon * first + cos_lon * second
    north_part = -sin_lat * cos_lon * first - sin_lat * sin_lon * second + cos_lat * third
    return (east_part, north_part)


def kernel(
    tiles, mems, blocks, slots, fine_blocks, fine_width, member_count,
    src_ref, cnt_ref, inc_hbm, ang_hbm, cang_hbm, mem_hbm, w_hbm,
    out_ref,
    inc_v, ang_v, cang_v, mem_v, w_v,
    cart, picked, req_out, req_in, rows_out, rows_in,
    part, part_in, delta,
    load_sem, w_sem, req_send, req_recv, rows_send, rows_recv,
    part_send, part_recv, delta_send, delta_recv,
):
    tile = lax.axis_index("tile")
    mem = lax.axis_index("mem")
    half = tiles // 2
    pairs = (slots - 2) // 2
    halves = fine_width // LANES
    own_rows = 2 * blocks
    wide = pairs * blocks

    loads = [
        pltpu.make_async_copy(inc_hbm, inc_v, load_sem.at[0]),
        pltpu.make_async_copy(ang_hbm, ang_v, load_sem.at[1]),
        pltpu.make_async_copy(
            cang_hbm.at[pl.ds(pl.multiple_of(mem * own_rows, own_rows), own_rows)], cang_v, load_sem.at[2]
        ),
        pltpu.make_async_copy(mem_hbm, mem_v, load_sem.at[3]),
    ]
    near_depth = 2 * fine_width
    near_load = pltpu.make_async_copy(
        w_hbm.at[:, pl.ds(0, near_depth)], w_v.at[:, pl.ds(0, near_depth)], w_sem.at[0]
    )
    far_depth = (slots - 2) * fine_width
    far_load = pltpu.make_async_copy(
        w_hbm.at[:, pl.ds(near_depth, far_depth)], w_v.at[:, pl.ds(near_depth, far_depth)], w_sem.at[1]
    )
    for load in loads:
        load.start()
    near_load.start()
    far_load.start()

    barrier = pltpu.get_barrier_semaphore()
    offsets = sorted({1, tiles - 1, half, tiles - half, half + 1, tiles - half - 1})
    for by in offsets:
        pl.semaphore_signal(
            barrier, inc=1, device_id=(mem, lax.rem(tile + by, tiles)), device_id_type=MESH
        )
    for by in range(1, mems):
        pl.semaphore_signal(
            barrier, inc=1, device_id=(lax.rem(mem + by, mems), tile), device_id_type=MESH
        )

    row = lax.broadcasted_iota(jnp.int32, (blocks, fine_blocks), 0)
    column = lax.broadcasted_iota(jnp.int32, (blocks, fine_blocks), 1)

    def ids_of(slot):
        ids = jnp.full((blocks, fine_blocks), -1, jnp.int32)
        for block in range(blocks):
            name = jnp.where(slot < cnt_ref[0, block], src_ref[slot, block], -1)
            ids = jnp.where(row == block, name, ids)
        return ids

    def pick(ids, shard):
        return jnp.where(column == ids - shard * fine_blocks, 1.0, 0.0).astype(jnp.bfloat16)

    lower = lax.rem(tile + tiles - 1, tiles)
    across = lax.rem(tile + half, tiles)
    beyond = lax.rem(tile + half + 1, tiles)
    own_picks = []
    for pair in range(pairs):
        below_ids = ids_of(2 + 2 * pair)
        across_ids = ids_of(3 + 2 * pair)
        at = slice(pair * blocks, (pair + 1) * blocks)
        req_out[0, at, :] = pick(below_ids, lower)
        req_out[1, at, :] = pick(across_ids, across)
        req_out[2, at, :] = pick(across_ids, beyond)
        own_picks.append(pick(below_ids, tile))
    pl.semaphore_wait(barrier, len(offsets) + mems - 1)

    asked = (lower, across, beyond)
    requests = []
    for flow in range(3):
        requests.append(
            pltpu.make_async_remote_copy(
                src_ref=req_out.at[flow], dst_ref=req_in.at[flow],
                send_sem=req_send.at[flow], recv_sem=req_recv.at[flow],
                device_id=(mem, asked[flow]), device_id_type=MESH,
            )
        )
        requests[-1].start()

    loads[0].wait()
    loads[1].wait()
    step = 32
    for start in range(0, fine_blocks, step):
        for part_at in range(halves):

            def taken(ref, component):
                first_row = start * 2 * halves + 2 * part_at + component
                return ref[pl.ds(first_row, step, stride=2 * halves), :]

            vector = to_vector(taken(inc_v, 0), taken(inc_v, 1), taken(ang_v, 0), taken(ang_v, 1))
            for component in range(3):
                left = component * fine_width + part_at * LANES
                cart[start : start + step, left : left + LANES] = vector[component].astype(jnp.bfloat16)

    served = (
        lax.rem(tile + 1, tiles),
        lax.rem(tile + tiles - half, tiles),
        lax.rem(tile + tiles - half - 1, tiles),
    )
    replies = []
    for flow in range(3):
        requests[flow].wait_recv()
        found = jnp.dot(req_in[flow], cart[...], preferred_element_type=jnp.float32).astype(jnp.bfloat16)
        for component in range(3):
            rows_out[flow, component * wide : (component + 1) * wide, :] = found[
                :, component * fine_width : (component + 1) * fine_width
            ]
        replies.append(
            pltpu.make_async_remote_copy(
                src_ref=rows_out.at[flow], dst_ref=rows_in.at[flow],
                send_sem=rows_send.at[flow], recv_sem=rows_recv.at[flow],
                device_id=(mem, served[flow]), device_id_type=MESH,
            )
        )
        replies[-1].start()

    loads[3].wait()
    part[...] = jnp.sum(mem_v[...], axis=0)
    sums = []
    for by in range(1, mems):
        peer = lax.rem(mem + by, mems)
        sums.append(
            pltpu.make_async_remote_copy(
                src_ref=part.at[pl.ds(pl.multiple_of(peer * own_rows, own_rows), own_rows)],
                dst_ref=part_in.at[by - 1],
                send_sem=part_send.at[by - 1], recv_sem=part_recv.at[by - 1],
                device_id=(peer, tile), device_id_type=MESH,
            )
        )
        sums[-1].start()

    local = jnp.concatenate([pick(ids_of(0), tile), pick(ids_of(1), tile)] + own_picks, axis=0)
    found = jnp.dot(local, cart[...], preferred_element_type=jnp.float32).astype(jnp.bfloat16)
    for order in range(2 + pairs):
        slot = order if order < 2 else 2 * order - 2
        for component in range(3):
            picked[
                component * blocks : (component + 1) * blocks, slot * fine_width : (slot + 1) * fine_width
            ] = found[
                order * blocks : (order + 1) * blocks, component * fine_width : (component + 1) * fine_width
            ]

    loads[2].wait()
    coarse_lon = cang_v[pl.ds(0, blocks, stride=2), :]
    coarse_lat = cang_v[pl.ds(1, blocks, stride=2), :]
    sin_lon, cos_lon = (jnp.sin(coarse_lon), jnp.cos(coarse_lon))
    sin_lat, cos_lat = (jnp.sin(coarse_lat), jnp.cos(coarse_lat))

    owner = lax.rem(lax.broadcasted_iota(jnp.int32, (3 * blocks, LANES), 0), blocks)

    def remap(left, depth):
        values = picked[:, left : left + depth]
        total = jnp.zeros((3 * blocks, LANES), jnp.float32)
        for block in range(blocks):
            product = jnp.dot(values, w_v[block, left : left + depth, :], preferred_element_type=jnp.float32)
            total = jnp.where(owner == block, product, total)
        return total

    near_load.wait()
    vector = remap(0, near_depth)

    for copy in sums:
        copy.wait_recv()
    mean = part[pl.ds(pl.multiple_of(mem * own_rows, own_rows), own_rows), :]
    for by in range(mems - 1):
        mean = mean + part_in[by]
    mean = mean / member_count

    far_load.wait()
    for flow in range(3):
        replies[flow].wait_recv()
    for pair in range(pairs):
        for component in range(3):
            rows = slice(component * blocks, (component + 1) * blocks)
            came = slice(component * wide + pair * blocks, component * wide + (pair + 1) * blocks)
            below_at = slice((2 + 2 * pair) * fine_width, (3 + 2 * pair) * fine_width)
            across_at = slice((3 + 2 * pair) * fine_width, (4 + 2 * pair) * fine_width)
            picked[rows, below_at] = picked[rows, below_at] + rows_in[0, came, :]
            picked[rows, across_at] = rows_in[1, came, :] + rows_in[2, came, :]
    vector = vector + remap(near_depth, far_depth)

    first, second, third = (vector[at * blocks : (at + 1) * blocks] for at in range(3))
    east = -sin_lon * first + cos_lon * second
    north = -sin_lat * cos_lon * first - sin_lat * sin_lon * second + cos_lat * third
    base = pl.multiple_of(mem * own_rows, own_rows)
    delta[pl.ds(base, blocks, stride=2), :] = east
    delta[pl.ds(base + 1, blocks, stride=2), :] = north
    mine = pl.ds(base, own_rows)
    delta[mine, :] = delta[mine, :] - mean
    shares = []
    for by in range(1, mems):
        shares.append(
            pltpu.make_async_remote_copy(
                src_ref=delta.at[mine], dst_ref=delta.at[mine],
                send_sem=delta_send.at[by - 1], recv_sem=delta_recv.at[by - 1],
                device_id=(lax.rem(mem + by, mems), tile), device_id_type=MESH,
            )
        )
        shares[-1].start()
    for copy in shares:
        copy.wait_recv()
    out_ref[...] = delta[...]
    for copy in requests + replies + sums + shares:
        copy.wait_send()


def interleaved(array):
    lead = array.shape[:-2]
    count = array.shape[-1] // LANES
    split = array.reshape(lead + (2, count, LANES))
    return jnp.swapaxes(split, -3, -2).reshape(lead + (2 * count, LANES))


def shards(members, increment, fine_angles, coarse_angles, remap_weights, sources, counts):
    weights = remap_weights[0]
    blocks, slots, fine_width, coarse_width = weights.shape
    fine_blocks = increment.shape[1] // fine_width
    tiles, mems = (lax.axis_size("tile"), lax.axis_size("mem"))
    pairs = (slots - 2) // 2
    weights = weights.reshape(blocks, slots * fine_width, coarse_width)
    columns = coarse_angles.shape[1]
    rows = 2 * columns // LANES
    fine_rows = 2 * increment.shape[1] // LANES
    group = members.shape[0]
    operands = (
        sources[0].T,
        counts,
        interleaved(increment),
        interleaved(fine_angles),
        interleaved(coarse_angles),
        interleaved(members),
        weights,
    )
    any_spec = pl.BlockSpec(memory_space=pl.ANY)
    smem_spec = pl.BlockSpec(memory_space=pltpu.SMEM)
    dma = pltpu.SemaphoreType.DMA
    others = mems - 1
    delta = pl.pallas_call(
        functools.partial(kernel, tiles, mems, blocks, slots, fine_blocks, fine_width, group * mems),
        out_shape=jax.ShapeDtypeStruct((rows, LANES), jnp.float32),
        in_specs=[smem_spec, smem_spec] + [any_spec] * 5,
        out_specs=pl.BlockSpec(memory_space=pltpu.VMEM),
        scratch_shapes=[
            pltpu.VMEM((fine_rows, LANES), jnp.float32),
            pltpu.VMEM((fine_rows, LANES), jnp.float32),
            pltpu.VMEM((2 * blocks, LANES), jnp.float32),
            pltpu.VMEM((group, rows, LANES), jnp.float32),
            pltpu.VMEM(weights.shape, jnp.bfloat16),
            pltpu.VMEM((fine_blocks, 3 * fine_width), jnp.bfloat16),
            pltpu.VMEM((3 * blocks, slots * fine_width), jnp.bfloat16),
            pltpu.VMEM((3, pairs * blocks, fine_blocks), jnp.bfloat16),
            pltpu.VMEM((3, pairs * blocks, fine_blocks), jnp.bfloat16),
            pltpu.VMEM((3, 3 * pairs * blocks, fine_width), jnp.bfloat16),
            pltpu.VMEM((3, 3 * pairs * blocks, fine_width), jnp.bfloat16),
            pltpu.VMEM((rows, LANES), jnp.float32),
            pltpu.VMEM((others, 2 * blocks, LANES), jnp.float32),
            pltpu.VMEM((rows, LANES), jnp.float32),
            dma((4,)), dma((2,)),
            dma((3,)), dma((3,)), dma((3,)), dma((3,)),
            dma((others,)), dma((others,)), dma((others,)), dma((others,)),
        ],
        compiler_params=pltpu.CompilerParams(collective_id=0, has_side_effects=True),
        name="remap",
    )(*operands)
    shift = jnp.swapaxes(delta.reshape(rows // 2, 2, LANES), 0, 1).reshape(2, columns)
    return members + shift[None]


def solution(mesh):
    in_specs = (
        P("mem", None, "tile"),
        P(None, "tile"),
        P(None, "tile"),
        P(None, "tile"),
        P("tile", "mem", None, None, None),
        P("tile", "mem", None),
        P("tile", "mem"),
    )
    out_specs = P("mem", None, "tile")
    return jax.shard_map(shards, mesh=mesh, in_specs=in_specs, out_specs=out_specs, check_vma=False)
```

time: 68 us -> 20.8 us (0.31)
  Pallas kernels: 0 us -> 18.7 us
  local copies, waits for them, and re-layouts: 15.6 us -> 0.01 us
  between operations: 13.7 us -> 0.02 us
  waiting for transfers between devices: 9.8 us -> 0 us
  starting transfers between devices: 8.33 us -> 0 us
  blocking collectives: 8.25 us -> 0 us
  other arithmetic: 8.94 us -> 1.93 us
  matrix products: 2.94 us -> 0 us
    pallas_call x0 -> x1, Pallas kernels: none -> 18.7 us  [shards(): pl.pallas_call(functools.partial(kernel, tiles, mems, blocks, slots, fine...]
    cos x3 -> x0, local copies, waits for them, and re-layouts: 10.1 us -> none  [the longest x2 10 us: to_vector(): sin_lon, cos_lon = (jnp.sin(longitude), jnp.cos(longitude))]
    ppermute x6 -> x0, starting transfers between devices: 8.33 us -> none  [shifted(): lax.ppermute(value, axis, [(i, (i + by) % length) for i in range(length)])]
    all_gather x1 -> x0, blocking collectives: 8.25 us -> none  [shards(): coarse_wind = lax.all_gather(own_wind, 'mem', axis=1, tiled=True)]
    psum x1 -> x0, waiting for transfers between devices: 5.56 us -> none  [shards(): member_total = lax.psum(jnp.sum(members, axis=0), 'mem')]
    ppermute x6 -> x0, waiting for transfers between devices: 4.23 us -> none  [shifted(): lax.ppermute(value, axis, [(i, (i + by) % length) for i in range(length)])]
    gather x6 -> x0, local copies, waits for them, and re-layouts: 3.02 us -> none  [the longest x4 2.36 us: serve(): jnp.take(flat_blocks, jnp.clip(asked_ids, 0, fine_blocks - 1), axis=0)]
    dot_general x1 -> x0, matrix products: 2.94 us -> none  [shards(): jnp.einsum('ikcf,ikfb->cib', picked, weights, preferred_element_type=jnp....]
  transfers between devices with their start and end apart: 7 -> 0, of which waited for: 4 -> 0; matrix products, arithmetic and copies ran while one was open for 34% -> 0% of each run, Pallas kernels for 0% -> 0%
where the time goes in v1:
time: 20.8 us; the launch traced here: 20.7 us
  Pallas kernels  18.7 us (90%)
  other arithmetic  1.93 us (9%)
    pallas_call x1, Pallas kernels, shards(): pl.pallas_call(functools.partial(kernel, tiles, mems, blocks, slots, fine...  18.7 us
    add x1, other arithmetic, shards(): return members + shift[None]  1.93 us

profile of v1, /device:TPU:0, one launch (start us, length us, event | category | flops | bytes accessed | tf_op | source)
XLA Modules:
  0.0 20.7 jit_solution(8558502129351049842)
XLA Ops:
  0.0 0.0 copy-start
  0.0 18.7 %remap.1 = f32[128,128]{1,0:T(8,128)} custom-call(s32[4,16]{1,0:T(4,128)} %bitcast.35, s32[1,16]{1,0:T(1,128)} %cnt_ref.1, f32[512,128]{1,0:T(8,128)} %bitcast.32, f32[512,128]{1,0:T(8,128)} %bitcast.33, f32[128,128]{1,0:T(8,128)} %bitcast.34, f32[10,128,128]{2,1,0:T(8,128)} %bitcast.30, bf16[16,1024,128]{2,1,0:T(8,128)(2,1)} %bitcast.29), custom_call_target="tpu_custom_call" | custom-call | tf_op jit(solution)/shard_map/remap/pallas_call | solution.py:278
  18.7 0.0 copy-done
  18.7 1.9 %broadcast_add_fusion = f32[10,2,8192]{2,1,0:T(2,128)} fusion(f32[10,2,8192]{2,1,0:T(2,128)S(1)} %copy-done, f32[2,8192]{1,0:T(2,128)} %bitcast.31), kind=kLoop, calls=%fused_computation | loop fusion | flops 163840 | bytes 1376256 | tf_op jit(solution)/shard_map/add | solution.py:306
Async XLA Ops:
  0.0 18.7 %copy-start = (f32[10,2,8192]{2,1,0:T(2,128)S(1)}, f32[10,2,8192]{2,1,0:T(2,128)}, u32[]{:S(2)}) copy-start(f32[10,2,8192]{2,1,0:T(2,128)} %param.7) | copy-start | bytes 1966084

commit v2 on v1

--- a/solution.py
+++ b/solution.py
@@ -30,11 +30,11 @@
 
 def kernel(
     tiles, mems, blocks, slots, fine_blocks, fine_width, member_count,
-    src_ref, cnt_ref, inc_hbm, ang_hbm, cang_hbm, mem_hbm, w_hbm,
-    out_ref,
-    inc_v, ang_v, cang_v, mem_v, w_v,
+    src_hbm, cnt_hbm, inc_hbm, ang_hbm, cang_hbm, mem_hbm, w_hbm,
+    delta, mem_v,
+    src_ref, cnt_ref, inc_v, ang_v, cang_v, w_v,
     cart, picked, req_out, req_in, rows_out, rows_in,
-    part, part_in, delta,
+    part, part_in, delta_in,
     load_sem, w_sem, req_send, req_recv, rows_send, rows_recv,
     part_send, part_recv, delta_send, delta_recv,
 ):
@@ -46,27 +46,6 @@
     own_rows = 2 * blocks
     wide = pairs * blocks
 
-    loads = [
-        pltpu.make_async_copy(inc_hbm, inc_v, load_sem.at[0]),
-        pltpu.make_async_copy(ang_hbm, ang_v, load_sem.at[1]),
-        pltpu.make_async_copy(
-            cang_hbm.at[pl.ds(pl.multiple_of(mem * own_rows, own_rows), own_rows)], cang_v, load_sem.at[2]
-        ),
-        pltpu.make_async_copy(mem_hbm, mem_v, load_sem.at[3]),
-    ]
-    near_depth = 2 * fine_width
-    near_load = pltpu.make_async_copy(
-        w_hbm.at[:, pl.ds(0, near_depth)], w_v.at[:, pl.ds(0, near_depth)], w_sem.at[0]
-    )
-    far_depth = (slots - 2) * fine_width
-    far_load = pltpu.make_async_copy(
-        w_hbm.at[:, pl.ds(near_depth, far_depth)], w_v.at[:, pl.ds(near_depth, far_depth)], w_sem.at[1]
-    )
-    for load in loads:
-        load.start()
-    near_load.start()
-    far_load.start()
-
     barrier = pltpu.get_barrier_semaphore()
     offsets = sorted({1, tiles - 1, half, tiles - half, half + 1, tiles - half - 1})
     for by in offsets:
@@ -77,6 +56,23 @@
         pl.semaphore_signal(
             barrier, inc=1, device_id=(lax.rem(mem + by, mems), tile), device_id_type=MESH
         )
+
+    base = pl.multiple_of(mem * own_rows, own_rows)
+    loads = [
+        pltpu.make_async_copy(src_hbm, src_ref, load_sem.at[0]),
+        pltpu.make_async_copy(cnt_hbm, cnt_ref, load_sem.at[1]),
+        pltpu.make_async_copy(inc_hbm, inc_v, load_sem.at[2]),
+        pltpu.make_async_copy(ang_hbm, ang_v, load_sem.at[3]),
+        pltpu.make_async_copy(cang_hbm.at[pl.ds(base, own_rows)], cang_v, load_sem.at[4]),
+        pltpu.make_async_copy(mem_hbm, mem_v, load_sem.at[5]),
+    ]
+    src_load, cnt_load, inc_load, ang_load, cang_load, mem_load = loads
+    w_loads = []
+    for slot in range(slots):
+        depth = pl.ds(slot * fine_width, fine_width)
+        w_loads.append(pltpu.make_async_copy(w_hbm.at[:, depth], w_v.at[:, depth], w_sem.at[slot]))
+    for load in loads + w_loads:
+        load.start()
 
     row = lax.broadcasted_iota(jnp.int32, (blocks, fine_blocks), 0)
     column = lax.broadcasted_iota(jnp.int32, (blocks, fine_blocks), 1)
@@ -91,6 +87,8 @@
     def pick(ids, shard):
         return jnp.where(column == ids - shard * fine_blocks, 1.0, 0.0).astype(jnp.bfloat16)
 
+    src_load.wait()
+    cnt_load.wait()
     lower = lax.rem(tile + tiles - 1, tiles)
     across = lax.rem(tile + half, tiles)
     beyond = lax.rem(tile + half + 1, tiles)
@@ -117,8 +115,8 @@
         )
         requests[-1].start()
 
-    loads[0].wait()
-    loads[1].wait()
+    inc_load.wait()
+    ang_load.wait()
     step = 32
     for start in range(0, fine_blocks, step):
         for part_at in range(halves):
@@ -154,7 +152,7 @@
         )
         replies[-1].start()
 
-    loads[3].wait()
+    mem_load.wait()
     part[...] = jnp.sum(mem_v[...], axis=0)
     sums = []
     for by in range(1, mems):
@@ -180,7 +178,7 @@
                 order * blocks : (order + 1) * blocks, component * fine_width : (component + 1) * fine_width
             ]
 
-    loads[2].wait()
+    cang_load.wait()
     coarse_lon = cang_v[pl.ds(0, blocks, stride=2), :]
     coarse_lat = cang_v[pl.ds(1, blocks, stride=2), :]
     sin_lon, cos_lon = (jnp.sin(coarse_lon), jnp.cos(coarse_lon))
@@ -188,50 +186,61 @@
 
     owner = lax.rem(lax.broadcasted_iota(jnp.int32, (3 * blocks, LANES), 0), blocks)
 
-    def remap(left, depth):
-        values = picked[:, left : left + depth]
-        total = jnp.zeros((3 * blocks, LANES), jnp.float32)
-        for block in range(blocks):
-            product = jnp.dot(values, w_v[block, left : left + depth, :], preferred_element_type=jnp.float32)
-            total = jnp.where(owner == block, product, total)
+    def remap(used, total):
+        for block in range(0, blocks, 2):
+            product = None
+            for slot in used:
+                depth = slice(slot * fine_width, (slot + 1) * fine_width)
+                both = jnp.concatenate([w_v[block, depth, :], w_v[block + 1, depth, :]], axis=1)
+                term = jnp.dot(picked[:, depth], both, preferred_element_type=jnp.float32)
+                product = term if product is None else product + term
+            width = product.shape[1] // 2
+            total = jnp.where(owner == block, total + product[:, :width], total)
+            total = jnp.where(owner == block + 1, total + product[:, width:], total)
         return total
 
-    near_load.wait()
-    vector = remap(0, near_depth)
+    for slot in range(2):
+        w_loads[slot].wait()
+    vector = remap((0, 1), jnp.zeros((3 * blocks, LANES), jnp.float32))
 
     for copy in sums:
         copy.wait_recv()
-    mean = part[pl.ds(pl.multiple_of(mem * own_rows, own_rows), own_rows), :]
+    mean = part[pl.ds(base, own_rows), :]
     for by in range(mems - 1):
         mean = mean + part_in[by]
     mean = mean / member_count
 
-    far_load.wait()
-    for flow in range(3):
-        replies[flow].wait_recv()
-    for pair in range(pairs):
-        for component in range(3):
-            rows = slice(component * blocks, (component + 1) * blocks)
-            came = slice(component * wide + pair * blocks, component * wide + (pair + 1) * blocks)
-            below_at = slice((2 + 2 * pair) * fine_width, (3 + 2 * pair) * fine_width)
-            across_at = slice((3 + 2 * pair) * fine_width, (4 + 2 * pair) * fine_width)
-            picked[rows, below_at] = picked[rows, below_at] + rows_in[0, came, :]
-            picked[rows, across_at] = rows_in[1, came, :] + rows_in[2, came, :]
-    vector = vector + remap(near_depth, far_depth)
+    def arrived(flows, first_slot):
+        for flow in flows:
+            replies[flow].wait_recv()
+        for pair in range(pairs):
+            w_loads[first_slot + 2 * pair].wait()
+            depth = slice((first_slot + 2 * pair) * fine_width, (first_slot + 2 * pair + 1) * fine_width)
+            for component in range(3):
+                rows = slice(component * blocks, (component + 1) * blocks)
+                came = slice(component * wide + pair * blocks, component * wide + (pair + 1) * blocks)
+                terms = [rows_in[flow, came, :] for flow in flows]
+                if first_slot == 2:
+                    terms.append(picked[rows, depth])
+                picked[rows, depth] = terms[0] + terms[1]
+
+    arrived((0,), 2)
+    vector = remap(range(2, slots, 2), vector)
+    arrived((1, 2), 3)
+    vector = remap(range(3, slots, 2), vector)
 
     first, second, third = (vector[at * blocks : (at + 1) * blocks] for at in range(3))
     east = -sin_lon * first + cos_lon * second
     north = -sin_lat * cos_lon * first - sin_lat * sin_lon * second + cos_lat * third
-    base = pl.multiple_of(mem * own_rows, own_rows)
-    delta[pl.ds(base, blocks, stride=2), :] = east
-    delta[pl.ds(base + 1, blocks, stride=2), :] = north
     mine = pl.ds(base, own_rows)
-    delta[mine, :] = delta[mine, :] - mean
+    delta_in[pl.ds(base, blocks, stride=2), :] = east
+    delta_in[pl.ds(base + 1, blocks, stride=2), :] = north
+    delta_in[mine, :] = delta_in[mine, :] - mean
     shares = []
     for by in range(1, mems):
         shares.append(
             pltpu.make_async_remote_copy(
-                src_ref=delta.at[mine], dst_ref=delta.at[mine],
+                src_ref=delta_in.at[mine], dst_ref=delta_in.at[mine],
                 send_sem=delta_send.at[by - 1], recv_sem=delta_recv.at[by - 1],
                 device_id=(lax.rem(mem + by, mems), tile), device_id_type=MESH,
             )
@@ -239,9 +248,19 @@
         shares[-1].start()
     for copy in shares:
         copy.wait_recv()
-    out_ref[...] = delta[...]
+    delta[...] = delta_in[...]
     for copy in requests + replies + sums + shares:
         copy.wait_send()
+
+
+def finish(mem_v, delta, out_hbm, ready, sem):
+    copies = []
+    for at in range(mem_v.shape[0]):
+        ready[at] = mem_v[at] + delta[...]
+        copies.append(pltpu.make_async_copy(ready.at[at], out_hbm.at[at], sem.at[at]))
+        copies[-1].start()
+    for copy in copies:
+        copy.wait()
 
 
 def interleaved(array):
@@ -272,19 +291,23 @@
         weights,
     )
     any_spec = pl.BlockSpec(memory_space=pl.ANY)
-    smem_spec = pl.BlockSpec(memory_space=pltpu.SMEM)
+    vmem_spec = pl.BlockSpec(memory_space=pltpu.VMEM)
     dma = pltpu.SemaphoreType.DMA
     others = mems - 1
-    delta = pl.pallas_call(
+    delta, held = pl.pallas_call(
         functools.partial(kernel, tiles, mems, blocks, slots, fine_blocks, fine_width, group * mems),
-        out_shape=jax.ShapeDtypeStruct((rows, LANES), jnp.float32),
-        in_specs=[smem_spec, smem_spec] + [any_spec] * 5,
-        out_specs=pl.BlockSpec(memory_space=pltpu.VMEM),
+        out_shape=(
+            pltpu.VMEM((rows, LANES), jnp.float32),
+            pltpu.VMEM((group, rows, LANES), jnp.float32),
+        ),
+        in_specs=[any_spec] * 7,
+        out_specs=(vmem_spec, vmem_spec),
         scratch_shapes=[
+            pltpu.SMEM((slots, blocks), jnp.int32),
+            pltpu.SMEM((1, blocks), jnp.int32),
             pltpu.VMEM((fine_rows, LANES), jnp.float32),
             pltpu.VMEM((fine_rows, LANES), jnp.float32),
             pltpu.VMEM((2 * blocks, LANES), jnp.float32),
-            pltpu.VMEM((group, rows, LANES), jnp.float32),
             pltpu.VMEM(weights.shape, jnp.bfloat16),
             pltpu.VMEM((fine_blocks, 3 * fine_width), jnp.bfloat16),
             pltpu.VMEM((3 * blocks, slots * fine_width), jnp.bfloat16),
@@ -295,15 +318,23 @@
             pltpu.VMEM((rows, LANES), jnp.float32),
             pltpu.VMEM((others, 2 * blocks, LANES), jnp.float32),
             pltpu.VMEM((rows, LANES), jnp.float32),
-            dma((4,)), dma((2,)),
+            dma((6,)), dma((slots,)),
             dma((3,)), dma((3,)), dma((3,)), dma((3,)),
             dma((others,)), dma((others,)), dma((others,)), dma((others,)),
         ],
         compiler_params=pltpu.CompilerParams(collective_id=0, has_side_effects=True),
         name="remap",
     )(*operands)
-    shift = jnp.swapaxes(delta.reshape(rows // 2, 2, LANES), 0, 1).reshape(2, columns)
-    return members + shift[None]
+    recentered = pl.pallas_call(
+        finish,
+        out_shape=jax.ShapeDtypeStruct((group, rows, LANES), jnp.float32),
+        in_specs=[vmem_spec, vmem_spec],
+        out_specs=any_spec,
+        scratch_shapes=[pltpu.VMEM((group, rows, LANES), jnp.float32), dma((group,))],
+        name="recenter",
+    )(*(pltpu.with_memory_space_constraint(array, pltpu.VMEM) for array in (held, delta)))
+    split = recentered.reshape(group, rows // 2, 2, LANES)
+    return jnp.swapaxes(split, 1, 2).reshape(members.shape)
 
 
 def solution(mesh):

time: 20.8 us -> 17.7 us (0.85)
  other arithmetic: 1.93 us -> 0 us
  Pallas kernels: 18.7 us -> 17.5 us
    pallas_call x1, Pallas kernels: 18.7 us -> 16.6 us  [shards(): pl.pallas_call(functools.partial(kernel, tiles, mems, blocks, slots, fine...]
    add x1 -> x0, other arithmetic: 1.93 us -> none  [shards(): return members + shift[None]]
    pallas_call x0 -> x1, Pallas kernels: none -> 0.92 us  [shards(): pl.pallas_call(finish, out_shape=jax.ShapeDtypeStruct((group, rows, LANES...]
where the time goes in v2:
time: 17.7 us; the launch traced here: 17.5 us
  Pallas kernels  17.5 us (99%)
    pallas_call x1, Pallas kernels, shards(): pl.pallas_call(functools.partial(kernel, tiles, mems, blocks, slots, fine...  16.6 us
    pallas_call x1, Pallas kernels, shards(): pl.pallas_call(finish, out_shape=jax.ShapeDtypeStruct((group, rows, LANES...  0.92 us

profile of v2, /device:TPU:0, one launch (start us, length us, event | category | flops | bytes accessed | tf_op | source)
XLA Modules:
  0.0 17.5 jit_solution(18003831166062054020)
XLA Ops:
  0.0 16.6 %remap.1 = (f32[128,128]{1,0:T(8,128)S(1)}, f32[10,128,128]{2,1,0:T(8,128)S(1)}) custom-call(s32[4,16]{1,0:T(4,128)} %bitcast.34, s32[1,16]{1,0:T(1,128)} %cnt_hbm.1, f32[512,128]{1,0:T(8,128)} %bitcast.31, f32[512,128]{1,0:T(8,128)} %bitcast.32, f32[128,128]{1,0:T(8,128)} %bitcast.33, f32[10,128,128]{2,1,0:T(8,128)} %bitcast.30, bf16[16,1024,128]{2,1,0:T(8,128)(2,1)} %bitcast.29), custom_call_target="tpu_custom_call" | custom-call | tf_op jit(solution)/shard_map/remap/pallas_call | solution.py:297
  16.6 0.9 %recenter.1 = f32[10,128,128]{2,1,0:T(8,128)} custom-call(f32[10,128,128]{2,1,0:T(8,128)S(1)} %get-tuple-element.7.mem_v, f32[128,128]{1,0:T(8,128)S(1)} %get-tuple-element.8.delta), custom_call_target="tpu_custom_call" | custom-call | tf_op jit(solution)/shard_map/recenter/pallas_call | solution.py:328

commit v3 on v2

--- a/solution.py
+++ b/solution.py
@@ -34,7 +34,7 @@
     delta, mem_v,
     src_ref, cnt_ref, inc_v, ang_v, cang_v, w_v,
     cart, picked, req_out, req_in, rows_out, rows_in,
-    part, part_in, delta_in,
+    part, part_in, delta_in, share,
     load_sem, w_sem, req_send, req_recv, rows_send, rows_recv,
     part_send, part_recv, delta_send, delta_recv,
 ):
@@ -235,20 +235,22 @@
     mine = pl.ds(base, own_rows)
     delta_in[pl.ds(base, blocks, stride=2), :] = east
     delta_in[pl.ds(base + 1, blocks, stride=2), :] = north
-    delta_in[mine, :] = delta_in[mine, :] - mean
+    delta[mine, :] = delta_in[mine, :] - mean
+    share[mine, :] = delta[mine, :].astype(jnp.bfloat16)
     shares = []
     for by in range(1, mems):
         shares.append(
             pltpu.make_async_remote_copy(
-                src_ref=delta_in.at[mine], dst_ref=delta_in.at[mine],
+                src_ref=share.at[mine], dst_ref=share.at[mine],
                 send_sem=delta_send.at[by - 1], recv_sem=delta_recv.at[by - 1],
                 device_id=(lax.rem(mem + by, mems), tile), device_id_type=MESH,
             )
         )
         shares[-1].start()
-    for copy in shares:
-        copy.wait_recv()
-    delta[...] = delta_in[...]
+    for by in range(1, mems):
+        shares[by - 1].wait_recv()
+        came = pl.ds(pl.multiple_of(lax.rem(mem + mems - by, mems) * own_rows, own_rows), own_rows)
+        delta[came, :] = share[came, :].astype(jnp.float32)
     for copy in requests + replies + sums + shares:
         copy.wait_send()
 
@@ -318,6 +320,7 @@
             pltpu.VMEM((rows, LANES), jnp.float32),
             pltpu.VMEM((others, 2 * blocks, LANES), jnp.float32),
             pltpu.VMEM((rows, LANES), jnp.float32),
+            pltpu.VMEM((rows, LANES), jnp.bfloat16),
             dma((6,)), dma((slots,)),
             dma((3,)), dma((3,)), dma((3,)), dma((3,)),
             dma((others,)), dma((others,)), dma((others,)), dma((others,)),

time: 17.7 us -> 17.5 us (0.989)
  Pallas kernels: 17.5 us -> 17.3 us
    pallas_call x1, Pallas kernels: 16.6 us -> 16.4 us  [shards(): pl.pallas_call(functools.partial(kernel, tiles, mems, blocks, slots, fine...]
where the time goes in v3:
time: 17.5 us; the launch traced here: 17.3 us
  Pallas kernels  17.3 us (99%)
    pallas_call x1, Pallas kernels, shards(): pl.pallas_call(functools.partial(kernel, tiles, mems, blocks, slots, fine...  16.4 us
    pallas_call x1, Pallas kernels, shards(): pl.pallas_call(finish, out_shape=jax.ShapeDtypeStruct((group, rows, LANES...  0.92 us

profile of v3, /device:TPU:0, one launch (start us, length us, event | category | flops | bytes accessed | tf_op | source)
XLA Modules:
  0.0 17.3 jit_solution(16639373625738487178)
XLA Ops:
  0.0 16.4 %remap.1 = (f32[128,128]{1,0:T(8,128)S(1)}, f32[10,128,128]{2,1,0:T(8,128)S(1)}) custom-call(s32[4,16]{1,0:T(4,128)} %bitcast.34, s32[1,16]{1,0:T(1,128)} %cnt_hbm.1, f32[512,128]{1,0:T(8,128)} %bitcast.31, f32[512,128]{1,0:T(8,128)} %bitcast.32, f32[128,128]{1,0:T(8,128)} %bitcast.33, f32[10,128,128]{2,1,0:T(8,128)} %bitcast.30, bf16[16,1024,128]{2,1,0:T(8,128)(2,1)} %bitcast.29), custom_call_target="tpu_custom_call" | custom-call | tf_op jit(solution)/shard_map/remap/pallas_call | solution.py:299
  16.4 0.9 %recenter.1 = f32[10,128,128]{2,1,0:T(8,128)} custom-call(f32[10,128,128]{2,1,0:T(8,128)S(1)} %get-tuple-element.7.mem_v, f32[128,128]{1,0:T(8,128)S(1)} %get-tuple-element.8.delta), custom_call_target="tpu_custom_call" | custom-call | tf_op jit(solution)/shard_map/recenter/pallas_call | solution.py:331

commit v4 on v3

--- a/solution.py
+++ b/solution.py
@@ -46,6 +46,10 @@
     own_rows = 2 * blocks
     wide = pairs * blocks
 
+    src_load = pltpu.make_async_copy(src_hbm, src_ref, load_sem.at[0])
+    cnt_load = pltpu.make_async_copy(cnt_hbm, cnt_ref, load_sem.at[1])
+    src_load.start()
+    cnt_load.start()
     barrier = pltpu.get_barrier_semaphore()
     offsets = sorted({1, tiles - 1, half, tiles - half, half + 1, tiles - half - 1})
     for by in offsets:
@@ -59,14 +63,12 @@
 
     base = pl.multiple_of(mem * own_rows, own_rows)
     loads = [
-        pltpu.make_async_copy(src_hbm, src_ref, load_sem.at[0]),
-        pltpu.make_async_copy(cnt_hbm, cnt_ref, load_sem.at[1]),
         pltpu.make_async_copy(inc_hbm, inc_v, load_sem.at[2]),
         pltpu.make_async_copy(ang_hbm, ang_v, load_sem.at[3]),
         pltpu.make_async_copy(cang_hbm.at[pl.ds(base, own_rows)], cang_v, load_sem.at[4]),
         pltpu.make_async_copy(mem_hbm, mem_v, load_sem.at[5]),
     ]
-    src_load, cnt_load, inc_load, ang_load, cang_load, mem_load = loads
+    inc_load, ang_load, cang_load, mem_load = loads
     w_loads = []
     for slot in range(slots):
         depth = pl.ds(slot * fine_width, fine_width)

time: 17.5 us -> 17.5 us (level)
  no operation moved by 1% of the time
where the time goes in v4:
time: 17.5 us; the launch traced here: 17.3 us
  Pallas kernels  17.3 us (99%)
    pallas_call x1, Pallas kernels, shards(): pl.pallas_call(functools.partial(kernel, tiles, mems, blocks, slots, fine...  16.4 us
    pallas_call x1, Pallas kernels, shards(): pl.pallas_call(finish, out_shape=jax.ShapeDtypeStruct((group, rows, LANES...  0.92 us

profile of v4, /device:TPU:0, one launch (start us, length us, event | category | flops | bytes accessed | tf_op | source)
XLA Modules:
  0.0 17.3 jit_solution(12897716256011523111)
XLA Ops:
  0.0 16.4 %remap.1 = (f32[128,128]{1,0:T(8,128)S(1)}, f32[10,128,128]{2,1,0:T(8,128)S(1)}) custom-call(s32[4,16]{1,0:T(4,128)} %bitcast.34, s32[1,16]{1,0:T(1,128)} %cnt_hbm.1, f32[512,128]{1,0:T(8,128)} %bitcast.31, f32[512,128]{1,0:T(8,128)} %bitcast.32, f32[128,128]{1,0:T(8,128)} %bitcast.33, f32[10,128,128]{2,1,0:T(8,128)} %bitcast.30, bf16[16,1024,128]{2,1,0:T(8,128)(2,1)} %bitcast.29), custom_call_target="tpu_custom_call" | custom-call | tf_op jit(solution)/shard_map/remap/pallas_call | solution.py:301
  16.4 0.9 %recenter.1 = f32[10,128,128]{2,1,0:T(8,128)} custom-call(f32[10,128,128]{2,1,0:T(8,128)S(1)} %get-tuple-element.7.mem_v, f32[128,128]{1,0:T(8,128)S(1)} %get-tuple-element.8.delta), custom_call_target="tpu_custom_call" | custom-call | tf_op jit(solution)/shard_map/recenter/pallas_call | solution.py:333
